TPU v7x, 32 devices: a whole 2x2x4 slice. The times are simulated.
32 devices in a mesh: ep: 16 (over z, y, core), rep: 2 (over x).
Axes of the slice: x: 2, y: 2, z: 4, core: 2. Of those that a mesh axis runs over, the one named last changes fastest.
Arguments:
- out_grad: bfloat16 [4096, 2048], P(('ep', 'rep')), may hold values from -6 to 6
- hidden: bfloat16 [4096, 8, 768], P(('ep', 'rep')), may hold values from -6 to 6
- expert_ids: int32 [4096, 8], P(('ep', 'rep')), may hold values from 0 to 15, all different within a row; in each aligned block of 128 rows (0 to 127, 128 to 255, ...) at most 72 rows name the same one
- gates: float32 [4096, 8], P(('ep', 'rep')), may hold values from 0.02 to 0.5
- weights: bfloat16 [16, 768, 2048], P('ep', 'rep'), may hold values from -0.125 to 0.125
- row_moment: float32 [16, 768], P('ep', 'rep'), may hold values from 16 to 1024
- col_moment: float32 [16, 2, 2048], P('ep', 'rep'), may hold values from 16 to 1024
Outputs:
- hidden_grad: bfloat16 [4096, 8, 768], P(('ep', 'rep'))
- update: bfloat16 [16, 768, 2048], P('ep', 'rep')
- row_new: float32 [16, 768], P('ep', 'rep')
- col_new: float32 [16, 2, 2048], P('ep', 'rep')
Inputs may be any that keep to these rules, and one draw needn't show every extreme that they name: `expert_ids`: the 8 experts of a token are distinct. Among the tokens of one device no expert is chosen more than 72 times, and in every draw some device reaches 72 for some expert.
All inputs are finite; a program needn't handle non-finite values.
Results may differ from a plain program's by a relative error of at most 0.014.
Values may be sent and summed in bfloat16 or wider, within the bound.
A program may use at most 128 MiB of HBM per device.

v0:
```python
import jax
import jax.numpy as jnp
from jax import lax
from jax.sharding import PartitionSpec as P

decay_rate = 0.9
epsilon = 1e-06


def local(out_grad, hidden, expert_ids, gates, weights, row_moment, col_moment):
    tok_rows, route_count = expert_ids.shape
    width = out_grad.shape[1]
    inner = hidden.shape[2]
    experts = lax.axis_size("ep")
    capacity = max(2, tok_rows * route_count * 9 // (8 * experts))
    routes = tok_rows * route_count
    flat_ids = expert_ids.reshape(routes)
    one_hot = (flat_ids[:, None] == jnp.arange(experts, dtype=jnp.int32)[None, :]).astype(jnp.int32)
    ranks = jnp.cumsum(one_hot, axis=0) - one_hot
    rank_own = jnp.sum(ranks * one_hot, axis=1)
    position = flat_ids * capacity + rank_own
    scaled = (
        (gates[:, :, None] * out_grad[:, None, :].astype(jnp.float32))
        .astype(jnp.bfloat16)
        .reshape(routes, width)
    )
    slots = experts * capacity
    send_scaled = jnp.zeros((slots, width), jnp.bfloat16).at[position].set(scaled)
    send_hidden = (
        jnp.zeros((slots, inner), jnp.bfloat16).at[position].set(hidden.reshape(routes, inner))
    )
    recv_scaled, recv_hidden = (
        lax.all_to_all(send_scaled, "ep", split_axis=0, concat_axis=0, tiled=True),
        lax.all_to_all(send_hidden, "ep", split_axis=0, concat_axis=0, tiled=True),
    )
    own_block = weights[0]
    input_grad = lax.dot_general(
        recv_scaled,
        lax.all_gather(own_block, "rep", axis=0, tiled=True),
        (((1,), (1,)), ((), ())),
        preferred_element_type=jnp.float32,
    ).astype(jnp.bfloat16)
    term = lax.dot_general(
        recv_hidden, recv_scaled, (((0,), (0,)), ((), ())), preferred_element_type=jnp.float32
    )
    gradient = lax.psum_scatter(
        lax.optimization_barrier(term.astype(jnp.bfloat16))
        .astype(jnp.float32)
        .astype(jnp.bfloat16),
        "rep",
        scatter_dimension=0,
        tiled=True,
    ).astype(jnp.float32)
    returned = lax.all_to_all(input_grad, "ep", split_axis=0, concat_axis=0, tiled=True)
    hidden_grad = returned[position].reshape(tok_rows, route_count, inner)
    squares = gradient * gradient
    row_new = decay_rate * row_moment[0] + (1.0 - decay_rate) * (
        jnp.mean(squares, axis=1) + epsilon
    )
    col_new = decay_rate * col_moment[0, 0] + (1.0 - decay_rate) * (
        jnp.mean(squares, axis=0) + epsilon
    )
    second = row_new[:, None] * col_new[None, :] / jnp.mean(row_new)
    update = (gradient * lax.rsqrt(second)).astype(jnp.bfloat16)
    return (hidden_grad, update[None], row_new[None], col_new[None, None])


def solution(mesh):
    return jax.shard_map(
        local,
        mesh=mesh,
        in_specs=(
            P(("ep", "rep"), None),
            P(("ep", "rep"), None, None),
            P(("ep", "rep"), None),
            P(("ep", "rep"), None),
            P("ep", "rep", None),
            P("ep", "rep"),
            P("ep", "rep", None),
        ),
        out_specs=(
            P(("ep", "rep"), None, None),
            P("ep", "rep", None),
            P("ep", "rep"),
            P("ep", "rep", None),
        ),
        check_vma=False,
    )
```

profile of v0, /device:TPU:8, one launch (start us, length us, event | category | flops | bytes accessed | tf_op | source)
XLA Modules:
  0.0 256.8 jit_solution(4397358027282598844)
XLA Ops:
  7.2 0.0 copy-start
  7.2 0.8 broadcast_multiply_fusion.1
  8.0 0.8 copy.14
  8.8 0.1 eq.29
  8.9 0.1 eq.25
  9.0 0.1 copy.13
  9.1 0.1 mul.126
  9.2 4.5 %reduce-window.6 = s32[16,8,128]{2,1,0:T(8,128)S(1)} reduce-window(s32[16,8,128]{2,1,0:T(8,128)S(1)} %fusion.17, s32[]{:T(128)} %constant.12.clone.1), window={size=1x1x128 pad=0_0x0_0x127_0}, to_apply=%region_0.0 | reduce-window | flops 2080768 | bytes 131076 | tf_op jit(solution)/shard_map/reduce-window
  13.7 0.1 slice.10
  13.8 0.1 copy.16
  13.9 0.1 copy.17
  14.0 0.1 broadcast_add_fusion
  14.2 0.0 copy-done
  14.2 0.0 copy-start.1
  14.2 6.6 %scatter_custom_fusion.1 = bf16[1152,768]{1,0:T(8,128)(2,1)} fusion(s32[1024]{0:T(1024)S(1)} %bitcast.55, bf16[128,8,768]{2,1,0:T(8,128)(2,1)S(1)} %copy-done, bf16[]{:T(256)} %constant.10.clone.1), kind=kCustom, calls=%fused_computation.18 | custom fusion | bytes 3342338 | tf_op jit(solution)/shard_map/scatter | solution.py:30
  20.7 0.0 copy-start.4
  20.7 6.4 %all-to-all-start.2 = ((bf16[16,72,768]{2,1,0:T(8,128)(2,1)}), bf16[16,72,768]{2,1,0:T(8,128)(2,1)}, u32[]{:S(2)}, u32[]{:S(2)}) async-start(bf16[16,72,768]{2,1,0:T(8,128)(2,1)} %bitcast.12), calls=%async_computation.2 | async-start | bytes 3538944 | tf_op jit(solution)/shard_map/all_to_all | solution.py:34
  27.2 0.0 copy-done.1
  27.2 0.1 convert_element_type.31
  27.3 0.0 copy-done.4
  27.3 0.1 copy.18
  27.4 0.1 mul.128
  27.5 9.8 %scatter_custom_fusion = bf16[1152,2048]{1,0:T(8,128)(2,1)} fusion(s32[1024]{0:T(1024)S(1)} %bitcast.56, f32[128,2048]{1,0:T(8,128)S(1)} %convert_element_type.31, f32[1024]{0:T(1024)S(1)} %mul.128, bf16[]{:T(256)} %constant.10.clone.1), kind=kCustom, calls=%fused_computation.6 | custom fusion | flops 4194304 | bytes 5771266 | tf_op jit(solution)/shard_map/scatter | solution.py:28
  37.2 28.7 %all-to-all-done.2 = bf16[16,72,768]{2,1,0:T(8,128)(2,1)} async-done(((bf16[16,72,768]{2,1,0:T(8,128)(2,1)}), bf16[16,72,768]{2,1,0:T(8,128)(2,1)}, u32[]{:S(2)}, u32[]{:S(2)}) %all-to-all-start.2) | async-done | bytes 1769504 | tf_op jit(solution)/shard_map/all_to_all | solution.py:34
  66.0 6.5 %all-to-all-start = ((bf16[16,72,2048]{2,1,0:T(8,128)(2,1)}), bf16[16,72,2048]{2,1,0:T(8,128)(2,1)}, u32[]{:S(2)}, u32[]{:S(2)}) async-start(bf16[16,72,2048]{2,1,0:T(8,128)(2,1)} %bitcast.47), calls=%async_computation | async-start | bytes 9437184 | tf_op jit(solution)/shard_map/all_to_all | solution.py:33
  72.4 0.0 all-gather.3.cloned.1.call-start
  72.5 0.7 all-gather.3.cloned.1.call-update
  73.2 0.2 reduce-scatter.2.cloned.1.call-start
  73.4 101.1 %all-to-all-done = bf16[16,72,2048]{2,1,0:T(8,128)(2,1)} async-done(((bf16[16,72,2048]{2,1,0:T(8,128)(2,1)}), bf16[16,72,2048]{2,1,0:T(8,128)(2,1)}, u32[]{:S(2)}, u32[]{:S(2)}) %all-to-all-start) | async-done | bytes 4718624 | tf_op jit(solution)/shard_map/all_to_all | solution.py:33
  174.5 8.8 %bitcast_convert_fusion = bf16[768,2048]{1,0:T(8,128)(2,1)} fusion(bf16[16,72,768]{2,1,0:T(8,128)(2,1)} %all-to-all-done.2, bf16[16,72,2048]{2,1,0:T(8,128)(2,1)} %all-to-all-done), kind=kOutput, calls=%fused_computation.5 | convolution fusion | flops 3625451520 | bytes 9633792 | tf_op jit(solution)/shard_map/dot_general | solution.py:43
  183.3 0.0 reduce-scatter.2.cloned.1.call-update
  183.3 0.0 all-gather.3.cloned.1.call-done
  183.4 8.4 %convolution_convert_fusion = bf16[1152,768]{1,0:T(8,128)(2,1)} fusion(bf16[1152,2048]{1,0:T(8,128)(2,1)} %bitcast.6, bf16[1,768,2048]{2,1,0:T(8,128)(2,1)} %all-gather.3.cloned.1.call-done), kind=kOutput, calls=%fused_computation.13 | convolution fusion | flops 3624763392 | bytes 9633792 | tf_op jit(solution)/shard_map/dot_general | solution.py:37
  191.8 0.0 copy-start.3
  191.8 6.6 %all-to-all-start.1 = ((bf16[16,72,768]{2,1,0:T(8,128)(2,1)}), bf16[16,72,768]{2,1,0:T(8,128)(2,1)S(1)}, u32[]{:S(2)}, u32[]{:S(2)}) async-start(bf16[16,72,768]{2,1,0:T(8,128)(2,1)} %bitcast.48), calls=%async_computation.1 | async-start | bytes 3538944 | tf_op jit(solution)/shard_map/all_to_all | solution.py:54
  198.4 0.0 copy-done.3
  198.4 38.8 %all-to-all-done.1 = bf16[16,72,768]{2,1,0:T(8,128)(2,1)S(1)} async-done(((bf16[16,72,768]{2,1,0:T(8,128)(2,1)}), bf16[16,72,768]{2,1,0:T(8,128)(2,1)S(1)}, u32[]{:S(2)}, u32[]{:S(2)}) %all-to-all-start.1) | async-done | bytes 1769504 | tf_op jit(solution)/shard_map/all_to_all | solution.py:54
  237.2 0.0 copy-start.2
  237.2 5.2 %gather_fusion = bf16[1024,768]{1,0:T(8,128)(2,1)} fusion(bf16[1152,768]{1,0:T(8,128)(2,1)S(1)} %bitcast.46, s32[1024]{0:T(1024)S(1)} %broadcast_clamp_fusion), kind=kCustom, calls=%fused_computation | custom fusion | bytes 3149824 | tf_op jit(solution)/shard_map/gather | solution.py:55
  242.4 0.0 reduce-scatter.2.cloned.1.call-done
  242.4 1.9 fusion.5
  244.3 0.0 copy-done.2
  244.3 0.6 fusion.20
  245.0 0.6 fusion.21
  245.6 0.6 reshape_add_fusion
  246.8 3.2 %fusion.10 = bf16[1,384,2048]{2,1,0:T(8,128)(2,1)} fusion(bf16[384,2048]{1,0:T(8,128)(2,1)} %reduce-scatter.2.cloned.1.call-done, f32[]{:T(128)S(6)} %div.25, f32[2048]{0:T(1024)S(1)} %fusion.19, f32[384]{0:T(512)S(1)} %get-tuple-element.7), kind=kLoop, calls=%fused_computation.17 | loop fusion | flops 3932160 | bytes 3155460 | tf_op jit(solution)/shard_map/broadcast_in_dim | solution.py:65
  (9 shorter events, 0.1 us)
Async XLA Ops:
  7.2 7.0 %copy-start = (bf16[128,8,768]{2,1,0:T(8,128)(2,1)S(1)}, bf16[128,8,768]{2,1,0:T(8,128)(2,1)}, u32[]{:S(2)}) copy-start(bf16[128,8,768]{2,1,0:T(8,128)(2,1)} %param.8) | copy-start | bytes 4718596
  14.2 13.0 %copy-start.1 = (bf16[128,2048]{1,0:T(8,128)(2,1)S(1)}, bf16[128,2048]{1,0:T(8,128)(2,1)}, u32[]{:S(2)}) copy-start(bf16[128,2048]{1,0:T(8,128)(2,1)} %param.7) | copy-start | bytes 1572868
  20.7 6.5 %copy-start.4 = (f32[128,8]{0,1:T(8,128)S(1)}, f32[128,8]{0,1:T(8,128)}, u32[]{:S(2)}) copy-start(f32[128,8]{0,1:T(8,128)} %param.10) | copy-start | bytes 12292
  20.7 45.3 %all-to-all-start.2 = ((bf16[16,72,768]{2,1,0:T(8,128)(2,1)}), bf16[16,72,768]{2,1,0:T(8,128)(2,1)}, u32[]{:S(2)}, u32[]{:S(2)}) async-start(bf16[16,72,768]{2,1,0:T(8,128)(2,1)} %bitcast.12), calls=%async_computation.2 | async-start | bytes 3538944 | tf_op jit(solution)/shard_map/all_to_all | solution.py:34
  66.0 108.5 %all-to-all-start = ((bf16[16,72,2048]{2,1,0:T(8,128)(2,1)}), bf16[16,72,2048]{2,1,0:T(8,128)(2,1)}, u32[]{:S(2)}, u32[]{:S(2)}) async-start(bf16[16,72,2048]{2,1,0:T(8,128)(2,1)} %bitcast.47), calls=%async_computation | async-start | bytes 9437184 | tf_op jit(solution)/shard_map/all_to_all | solution.py:33
  72.4 110.9 %all-gather.3.cloned.1.call-start = ((), (), s32[]{:S(2)}) async-start(), calls=%async_computation.5 | async-start | bytes 4718592 | tf_op jit(solution)/shard_map/all_gather | solution.py:39
  73.2 169.2 %reduce-scatter.2.cloned.1.call-start = ((), (), s32[]{:S(2)}) async-start(), calls=%async_computation.4 | async-start | bytes 4718592 | tf_op jit(solution)/shard_map/reduce_scatter | solution.py:46
  191.8 6.6 %copy-start.3 = (f32[1,384]{1,0:T(1,128)S(1)}, f32[1,384]{1,0:T(1,128)}, u32[]{:S(2)}) copy-start(f32[1,384]{1,0:T(1,128)} %param.12) | copy-start | bytes 4612
  191.8 45.4 %all-to-all-start.1 = ((bf16[16,72,768]{2,1,0:T(8,128)(2,1)}), bf16[16,72,768]{2,1,0:T(8,128)(2,1)S(1)}, u32[]{:S(2)}, u32[]{:S(2)}) async-start(bf16[16,72,768]{2,1,0:T(8,128)(2,1)} %bitcast.48), calls=%async_computation.1 | async-start | bytes 3538944 | tf_op jit(solution)/shard_map/all_to_all | solution.py:54
  237.2 7.1 %copy-start.2 = (f32[1,1,2048]{2,1,0:T(1,128)S(1)}, f32[1,1,2048]{2,1,0:T(1,128)}, u32[]{:S(2)}) copy-start(f32[1,1,2048]{2,1,0:T(1,128)} %param.13) | copy-start | bytes 24580
Sparse Core Ops, SparseCore 0:
  74.8 45.7 all-gather.2
  183.4 44.7 reduce-scatter.1
where the time goes:
time: 259 us; the launch traced here: 257 us
  waiting for transfers between devices  169 us (65%)
  other arithmetic  22.2 us (9%)
  starting transfers between devices  19.7 us (8%)
  matrix products  17.3 us (7%)
  between operations  14.8 us (6%)
  local copies, waits for them, and re-layouts  13.4 us (5%)
    all_to_all x1, waiting for transfers between devices, local(): lax.all_to_all(send_scaled, 'ep', split_axis=0, concat_axis=0, tiled=True)  101 us
    all_to_all x1, waiting for transfers between devices, local(): lax.all_to_all(input_grad, 'ep', split_axis=0, concat_axis=0, tiled=True)  38.8 us
    all_to_all x1, waiting for transfers between devices, local(): lax.all_to_all(send_hidden, 'ep', split_axis=0, concat_axis=0, tiled=True)  28.7 us
    scatter x1, other arithmetic, local(): jnp.zeros((slots, width), jnp.bfloat16).at[position].set(scaled)  9.76 us
    dot_general x1, matrix products, local(): lax.dot_general(recv_hidden, recv_scaled, (((0,), (0,)), ((), ())), prefe...  8.83 us
    dot_general x1, matrix products, local(): lax.dot_general(recv_scaled, lax.all_gather(own_block, 'rep', axis=0, til...  8.44 us
    all_to_all x1, starting transfers between devices, local(): lax.all_to_all(input_grad, 'ep', split_axis=0, concat_axis=0, tiled=True)  6.59 us
    scatter x1, local copies, waits for them, and re-layouts, local(): jnp.zeros((slots, inner), jnp.bfloat16).at[position]  6.55 us
  transfers between devices with their start and end apart: 5, of which 3 were waited for; matrix products, arithmetic and copies ran while one was open for 13% of the time, Pallas kernels for 0%

commit v1 on v0

v1 whole, which is shorter than its diff:
```python
import jax
import jax.numpy as jnp
from jax import lax
from jax.sharding import PartitionSpec as P

decay_rate = 0.9
epsilon = 1e-06


def local(out_grad, hidden, expert_ids, gates, weights, row_moment, col_moment):
    tok_rows, route_count = expert_ids.shape
    inner = hidden.shape[2]
    experts = lax.axis_size("ep")
    capacity = max(2, tok_rows * route_count * 9 // (8 * experts))
    routes = tok_rows * route_count
    slots = experts * capacity

    gathered = lax.all_gather(out_grad, "ep", axis=0, tiled=False)
    weight = lax.all_gather(weights[0], "rep", axis=0, tiled=True)

    hit = expert_ids[:, :, None] == jnp.arange(experts, dtype=jnp.int32)
    chosen = jnp.any(hit, axis=1)
    before = jnp.tril(jnp.ones((tok_rows, tok_rows), jnp.bfloat16), -1)
    rank = jnp.dot(
        before, chosen.astype(jnp.bfloat16), preferred_element_type=jnp.float32
    ).astype(jnp.int32)
    place = jnp.where(chosen, rank, -1).T
    place_in = lax.all_to_all(place, "ep", split_axis=0, concat_axis=0, tiled=True)

    rank_own = jnp.sum(jnp.where(hit, rank[:, None, :], 0), axis=2)
    position = (expert_ids * capacity + rank_own).reshape(routes)

    gated = (
        (gates[:, :, None] * hidden.astype(jnp.float32))
        .astype(jnp.bfloat16)
        .reshape(routes, inner)
    )
    send_hidden = jnp.zeros((slots, inner), jnp.bfloat16).at[position].set(gated)
    recv_hidden = lax.all_to_all(send_hidden, "ep", split_axis=0, concat_axis=0, tiled=True)

    pick = (place_in[:, None, :] == jnp.arange(capacity, dtype=jnp.int32)[None, :, None]).astype(
        jnp.bfloat16
    )
    rows = (
        jnp.einsum("sjt,std->sjd", pick, gathered, preferred_element_type=jnp.float32)
        .astype(jnp.bfloat16)
        .reshape(slots, -1)
    )
    input_grad = lax.dot_general(
        rows, weight, (((1,), (1,)), ((), ())), preferred_element_type=jnp.float32
    ).astype(jnp.bfloat16)
    returned = lax.all_to_all(input_grad, "ep", split_axis=0, concat_axis=0, tiled=True)
    term = lax.dot_general(
        recv_hidden, rows, (((0,), (0,)), ((), ())), preferred_element_type=jnp.float32
    )
    gradient = lax.psum_scatter(
        term.astype(jnp.bfloat16), "rep", scatter_dimension=0, tiled=True
    ).astype(jnp.float32)
    hidden_grad = (
        gates[:, :, None]
        * returned[position].reshape(tok_rows, route_count, inner).astype(jnp.float32)
    ).astype(jnp.bfloat16)
    squares = gradient * gradient
    row_new = decay_rate * row_moment[0] + (1.0 - decay_rate) * (
        jnp.mean(squares, axis=1) + epsilon
    )
    col_new = decay_rate * col_moment[0, 0] + (1.0 - decay_rate) * (
        jnp.mean(squares, axis=0) + epsilon
    )
    second = row_new[:, None] * col_new[None, :] / jnp.mean(row_new)
    update = (gradient * lax.rsqrt(second)).astype(jnp.bfloat16)
    return (hidden_grad, update[None], row_new[None], col_new[None, None])


def solution(mesh):
    return jax.shard_map(
        local,
        mesh=mesh,
        in_specs=(
            P(("ep", "rep"), None),
            P(("ep", "rep"), None, None),
            P(("ep", "rep"), None),
            P(("ep", "rep"), None),
            P("ep", "rep", None),
            P("ep", "rep"),
            P("ep", "rep", None),
        ),
        out_specs=(
            P(("ep", "rep"), None, None),
            P("ep", "rep", None),
            P("ep", "rep"),
            P("ep", "rep", None),
        ),
        check_vma=False,
    )
```

time: 259 us -> 235 us (0.907)
  waiting for transfers between devices: 169 us -> 152 us
  local copies, waits for them, and re-layouts: 13.4 us -> 5 us
  matrix products: 17.3 us -> 24.3 us
  other arithmetic: 22.2 us -> 17.9 us
    all_gather x1 -> x2, waiting for transfers between devices: 0.02 us -> 112 us  [the longest x1 79.4 us: local(): gathered = lax.all_gather(out_grad, 'ep', axis=0, tiled=False)]
    all_to_all x1, waiting for transfers between devices: 101 us -> 0.01 us  [local(): lax.all_to_all(place, 'ep', split_axis=0, concat_axis=0, tiled=True)]
    all_to_all x1, waiting for transfers between devices: 28.7 us -> 0.01 us  [local(): lax.all_to_all(send_hidden, 'ep', split_axis=0, concat_axis=0, tiled=True)]
    dot_general x2 -> x4, matrix products: 17.3 us -> 24.3 us  [the longest x1 8.42 us: local(): lax.dot_general(rows, weight, (((1,), (1,)), ((), ())), preferred_element...]
    scatter x1 -> x0, local copies, waits for them, and re-layouts: 6.55 us -> none  [local(): jnp.zeros((slots, inner), jnp.bfloat16).at[position]]
    another operation x3 -> x0, other arithmetic: 4.64 us -> none
  transfers between devices with their start and end apart: 5 -> 6, of which waited for: 3 -> 3; matrix products, arithmetic and copies ran while one was open for 13% -> 17% of each run, Pallas kernels for 0% -> 0%
where the time goes in v1:
time: 235 us; the launch traced here: 232 us
  waiting for transfers between devices  152 us (65%)
  matrix products  24.3 us (10%)
  starting transfers between devices  18.6 us (8%)
  other arithmetic  17.9 us (8%)
  between operations  14.5 us (6%)
  local copies, waits for them, and re-layouts  5 us (2%)
    all_gather x1, waiting for transfers between devices, local(): gathered = lax.all_gather(out_grad, 'ep', axis=0, tiled=False)  79.4 us
    all_to_all x1, waiting for transfers between devices, local(): lax.all_to_all(input_grad, 'ep', split_axis=0, concat_axis=0, tiled=True)  38.8 us
    all_gather x1, waiting for transfers between devices, local(): weight = lax.all_gather(weights[0], 'rep', axis=0, tiled=True)  32.4 us
    dot_general x1, matrix products, local(): lax.dot_general(rows, weight, (((1,), (1,)), ((), ())), preferred_element...  8.42 us
    dot_general x1, matrix products, local(): lax.dot_general(recv_hidden, rows, (((0,), (0,)), ((), ())), preferred_el...  8.19 us
    scatter x1, other arithmetic, local(): jnp.zeros((slots, inner), jnp.bfloat16).at[position].set(gated)  7.4 us
    dot_general x1, matrix products, local(): jnp.einsum('sjt,std->sjd', pick, gathered, preferred_element_type=jnp.flo...  6.91 us
    all_to_all x1, starting transfers between devices, local(): lax.all_to_all(place, 'ep', split_axis=0, concat_axis=0, tiled=True)  6.3 us
  transfers between devices with their start and end apart: 6, of which 3 were waited for; matrix products, arithmetic and copies ran while one was open for 17% of the time, Pallas kernels for 0%

profile of v1, /device:TPU:8, one launch (start us, length us, event | category | flops | bytes accessed | tf_op | source)
XLA Modules:
  0.0 232.3 jit_solution(6559132608907882954)
XLA Ops:
  7.2 0.0 all-gather.5.cloned.1.call-start
  7.2 0.7 all-gather.5.cloned.1.call-update
  7.9 0.7 fusion.12
  8.6 0.8 broadcast_select_fusion
  9.4 6.3 %all-to-all-start = ((s32[16,1,128]{2,1,0:T(1,128)}), s32[16,1,128]{2,1,0:T(1,128)S(1)}, u32[]{:S(2)}, u32[]{:S(2)}) async-start(s32[16,1,128]{2,1,0:T(1,128)} %bitcast.2), calls=%async_computation | async-start | bytes 16384 | tf_op jit(solution)/shard_map/all_to_all | solution.py:28
  15.7 0.7 select_reduce_fusion
  16.4 0.7 multiply_add_fusion
  17.1 0.1 copy.25
  17.2 0.1 reshape.124
  17.3 0.8 copy.23
  18.1 7.4 %scatter_custom_fusion = bf16[1152,768]{1,0:T(8,128)(2,1)} fusion(s32[1024]{0:T(1024)S(1)} %bitcast.38, bf16[128,8,768]{2,1,0:T(8,128)(2,1)} %param.8, f32[128,8]{1,0:T(8,128)S(1)} %copy.23, bf16[]{:T(256)} %constant.16.clone.1), kind=kCustom, calls=%fused_computation.15 | custom fusion | flops 2359296 | bytes 3407874 | tf_op jit(solution)/shard_map/scatter | solution.py:38
  25.5 0.0 all-to-all-done
  25.5 6.0 %all-to-all-start.2 = ((bf16[16,72,768]{2,1,0:T(8,128)(2,1)}), bf16[16,72,768]{2,1,0:T(8,128)(2,1)S(1)}, u32[]{:S(2)}, u32[]{:S(2)}) async-start(bf16[16,72,768]{2,1,0:T(8,128)(2,1)} %bitcast.12), calls=%async_computation.2 | async-start | bytes 3538944 | tf_op jit(solution)/shard_map/all_to_all | solution.py:39
  31.6 0.0 all-gather.7.cloned.1.call-start
  31.6 0.7 all-gather.7.cloned.1.call-update
  32.3 0.0 reduce-scatter.2.cloned.1.call-start
  32.4 79.4 %all-gather.5.cloned.1.call-done = bf16[2048,2048]{1,0:T(8,128)(2,1)} async-done(((bf16[128,2048]{1,0:T(8,128)(2,1)}), bf16[2048,2048]{1,0:T(8,128)(2,1)}) %all-gather.5.cloned.1.call-update) | async-done | bytes 8388624 | tf_op jit(solution)/shard_map/all_gather | solution.py:18
  111.8 6.9 %convolution_convert_fusion = bf16[16,72,2048]{2,1,0:T(8,128)(2,1)} fusion(bf16[16,128,2048]{2,1,0:T(8,128)(2,1)} %bitcast.33, s32[16,128]{1,0:T(8,128)S(1)} %bitcast.35), kind=kOutput, calls=%fused_computation.3 | convolution fusion | flops 606486528 | bytes 13115392 | tf_op jit(solution)/shard_map/sjt,std->sjd/dot_general | solution.py:45
  118.7 0.0 all-to-all-done.2
  118.7 8.2 %bitcast_convert_fusion = bf16[768,2048]{1,0:T(8,128)(2,1)} fusion(bf16[16,72,768]{2,1,0:T(8,128)(2,1)S(1)} %all-to-all-done.2, bf16[16,72,2048]{2,1,0:T(8,128)(2,1)} %convolution_convert_fusion), kind=kOutput, calls=%fused_computation.2 | convolution fusion | flops 3625451520 | bytes 9633792 | tf_op jit(solution)/shard_map/dot_general | solution.py:53
  126.9 0.0 reduce-scatter.2.cloned.1.call-update
  126.9 32.4 %all-gather.7.cloned.1.call-done = bf16[1,768,2048]{2,1,0:T(8,128)(2,1)} async-done(((bf16[1,384,2048]{2,1,0:T(8,128)(2,1)}), bf16[1,768,2048]{2,1,0:T(8,128)(2,1)}) %all-gather.7.cloned.1.call-update) | async-done | bytes 3145744 | tf_op jit(solution)/shard_map/all_gather | solution.py:19
  159.3 8.4 %convolution_convert_fusion.1 = bf16[1152,768]{1,0:T(8,128)(2,1)} fusion(bf16[1152,2048]{1,0:T(8,128)(2,1)} %bitcast.34, bf16[1,768,2048]{2,1,0:T(8,128)(2,1)} %all-gather.7.cloned.1.call-done), kind=kOutput, calls=%fused_computation.8 | convolution fusion | flops 3624763392 | bytes 9633792 | tf_op jit(solution)/shard_map/dot_general | solution.py:49
  167.8 0.0 copy-start.1
  167.8 6.2 %all-to-all-start.1 = ((bf16[16,72,768]{2,1,0:T(8,128)(2,1)}), bf16[16,72,768]{2,1,0:T(8,128)(2,1)S(1)}, u32[]{:S(2)}, u32[]{:S(2)}) async-start(bf16[16,72,768]{2,1,0:T(8,128)(2,1)} %bitcast.7), calls=%async_computation.1 | async-start | bytes 3538944 | tf_op jit(solution)/shard_map/all_to_all | solution.py:52
  174.0 0.0 copy-done.1
  174.0 38.8 %all-to-all-done.1 = bf16[16,72,768]{2,1,0:T(8,128)(2,1)S(1)} async-done(((bf16[16,72,768]{2,1,0:T(8,128)(2,1)}), bf16[16,72,768]{2,1,0:T(8,128)(2,1)S(1)}, u32[]{:S(2)}, u32[]{:S(2)}) %all-to-all-start.1) | async-done | bytes 1769504 | tf_op jit(solution)/shard_map/all_to_all | solution.py:52
  212.8 4.0 %gather_fusion = bf16[1024,768]{1,0:T(8,128)(2,1)S(1)} fusion(bf16[1152,768]{1,0:T(8,128)(2,1)S(1)} %bitcast.32, s32[1024]{0:T(1024)S(1)} %broadcast_clamp_fusion), kind=kCustom, calls=%fused_computation | custom fusion | bytes 3149824 | tf_op jit(solution)/shard_map/gather | solution.py:61
  216.8 0.0 copy-start
  216.8 1.5 fusion.3
  218.3 0.0 reduce-scatter.2.cloned.1.call-done
  218.3 1.9 fusion
  220.2 0.0 copy-done
  220.2 0.6 fusion.22
  220.8 0.6 fusion.23
  221.4 0.6 reshape_add_fusion
  222.6 3.2 %fusion.8 = bf16[1,384,2048]{2,1,0:T(8,128)(2,1)} fusion(bf16[384,2048]{1,0:T(8,128)(2,1)} %reduce-scatter.2.cloned.1.call-done, f32[]{:T(128)S(6)} %div.25, f32[2048]{0:T(1024)S(1)} %fusion.21, f32[384]{0:T(512)S(1)} %get-tuple-element.7), kind=kLoop, calls=%fused_computation.16 | loop fusion | flops 3932160 | bytes 3155460 | tf_op jit(solution)/shard_map/broadcast_in_dim | solution.py:72
  (6 shorter events, 0.0 us)
Async XLA Ops:
  7.2 104.6 %all-gather.5.cloned.1.call-start = ((), (), s32[]{:S(2)}) async-start(), calls=%async_computation.5 | async-start | bytes 8912896 | tf_op jit(solution)/shard_map/all_gather | solution.py:18
  9.4 16.1 %all-to-all-start = ((s32[16,1,128]{2,1,0:T(1,128)}), s32[16,1,128]{2,1,0:T(1,128)S(1)}, u32[]{:S(2)}, u32[]{:S(2)}) async-start(s32[16,1,128]{2,1,0:T(1,128)} %bitcast.2), calls=%async_computation | async-start | bytes 16384 | tf_op jit(solution)/shard_map/all_to_all | solution.py:28
  25.5 93.2 %all-to-all-start.2 = ((bf16[16,72,768]{2,1,0:T(8,128)(2,1)}), bf16[16,72,768]{2,1,0:T(8,128)(2,1)S(1)}, u32[]{:S(2)}, u32[]{:S(2)}) async-start(bf16[16,72,768]{2,1,0:T(8,128)(2,1)} %bitcast.12), calls=%async_computation.2 | async-start | bytes 3538944 | tf_op jit(solution)/shard_map/all_to_all | solution.py:39
  31.6 127.8 %all-gather.7.cloned.1.call-start = ((), (), s32[]{:S(2)}) async-start(), calls=%async_computation.6 | async-start | bytes 4718592 | tf_op jit(solution)/shard_map/all_gather | solution.py:19
  32.3 186.0 %reduce-scatter.2.cloned.1.call-start = ((), (), s32[]{:S(2)}) async-start(), calls=%async_computation.4 | async-start | bytes 4718592 | tf_op jit(solution)/shard_map/reduce_scatter | solution.py:56
  167.8 6.2 %copy-start.1 = (f32[1,384]{1,0:T(1,128)S(1)}, f32[1,384]{1,0:T(1,128)}, u32[]{:S(2)}) copy-start(f32[1,384]{1,0:T(1,128)} %param.12) | copy-start | bytes 4612
  167.8 45.0 %all-to-all-start.1 = ((bf16[16,72,768]{2,1,0:T(8,128)(2,1)}), bf16[16,72,768]{2,1,0:T(8,128)(2,1)S(1)}, u32[]{:S(2)}, u32[]{:S(2)}) async-start(bf16[16,72,768]{2,1,0:T(8,128)(2,1)} %bitcast.7), calls=%async_computation.1 | async-start | bytes 3538944 | tf_op jit(solution)/shard_map/all_to_all | solution.py:52
  216.8 3.4 %copy-start = (f32[1,1,2048]{2,1,0:T(1,128)S(1)}, f32[1,1,2048]{2,1,0:T(1,128)}, u32[]{:S(2)}) copy-start(f32[1,1,2048]{2,1,0:T(1,128)} %param.13) | copy-start | bytes 24580
Sparse Core Ops, SparseCore 0:
  10.1 101.6 all-gather.4
  113.3 45.9 all-gather.6
  161.6 43.4 reduce-scatter.1

commit v2 on v1

v2 whole, which is shorter than its diff:
```python
import functools

import jax
import jax.numpy as jnp
from jax import lax
from jax.experimental import pallas as pl
from jax.experimental.pallas import tpu as pltpu
from jax.sharding import PartitionSpec as P

decay_rate = 0.9
epsilon = 1e-06
MESH = pl.DeviceIdType.MESH


def up_to(value, step):
    return -(-value // step) * step


def kernel(
    dims,
    og_ref,
    gated_ref,
    slot_ref,
    place_ref,
    w_ref,
    rowm_ref,
    colm_ref,
    returned_ref,
    update_ref,
    rown_ref,
    coln_ref,
    og_all,
    place_all,
    hsend,
    hrecv,
    rows,
    igbuf,
    wfull,
    parts,
    grad,
    og_recv,
    up_sem,
    down_sem,
    y_sem,
    core_sem,
    pl_send,
    pl_recv,
    h_send,
    h_recv,
    r_send,
    r_recv,
    w_send,
    w_recv,
    g_send,
    g_recv,
):
    n_ep, n_rep, outer, sent, cap, chunks = dims
    tok, width = og_ref.shape
    inner = gated_ref.shape[1]
    own_rows = inner // n_rep
    wide = width // chunks
    term = wfull
    me = lax.axis_index("ep")
    rep = lax.axis_index("rep")
    z, y, c = me // 4, (me // 2) % 2, me % 2
    y_dev = z * 4 + (1 - y) * 2 + c
    c_dev = z * 4 + y * 2 + (1 - c)
    way = 1 - 2 * (z // (outer // 2))

    og_all[me] = og_ref[...]
    wfull[rep] = w_ref[...]
    place_all[me] = place_ref[me]
    hrecv[...] = jnp.zeros_like(hrecv)

    barrier = pltpu.get_barrier_semaphore()
    for d in range(1, n_ep):
        pl.semaphore_signal(
            barrier, inc=1, device_id={"ep": lax.rem(me + d, n_ep)}, device_id_type=MESH
        )
    for d in range(1, n_rep):
        pl.semaphore_signal(
            barrier, inc=1, device_id={"rep": lax.rem(rep + d, n_rep)}, device_id_type=MESH
        )
    pl.semaphore_wait(barrier, n_ep - 1 + n_rep - 1)

    def remote(src, dst, send, recv, **where):
        return pltpu.make_async_remote_copy(
            src_ref=src, dst_ref=dst, send_sem=send, recv_sem=recv,
            device_id=where, device_id_type=MESH,
        )

    def og_copy(block, send, to, own):
        src = og_ref if own else og_all.at[block]
        return remote(src, og_all.at[block], send, og_recv.at[block], ep=to)

    def og_wait(block):
        remote(og_all.at[block], og_all.at[block], up_sem.at[0], og_recv.at[block], ep=me).wait_recv()

    def fan(zs, k, act):
        block = zs * 4 + y * 2 + c
        act(og_copy(block, y_sem.at[zs], y_dev, k == 0))
        act(og_copy(block, core_sem.at[zs * 2], c_dev, k == 0))

    def rise(zs, k, act):
        block = zs * 4 + y * 2 + c

        @pl.when(z + 1 < outer)
        def _():
            act(og_copy(block, up_sem.at[zs], me + 4, k == 0))

    def sink(zs, k, act):
        block = zs * 4 + y * 2 + c

        @pl.when(z > 0)
        def _():
            act(og_copy(block, down_sem.at[zs], me - 4, k == 0))

    def cross(zs, act):
        block = zs * 4 + (1 - y) * 2 + c
        act(og_copy(block, core_sem.at[zs * 2 + 1], c_dev, False))

    start = lambda copy: copy.start()
    finish = lambda copy: copy.wait_send()

    def own_sends(act):
        rise(z, 0, act)
        sink(z, 0, act)
        fan(z, 0, act)

    def forward(k, act, arrive):
        low, high = z - k, z + k

        @pl.when(low >= 0)
        def _():
            if arrive:
                og_wait(low * 4 + y * 2 + c)
            rise(low, k, act)
            fan(low, k, act)

        @pl.when(high < outer)
        def _():
            if arrive:
                og_wait(high * 4 + y * 2 + c)
            sink(high, k, act)
            fan(high, k, act)

    def crossing(k, act, arrive):
        for zs, ok in ((z - k, z - k >= 0), (z + k, z + k < outer))[: 1 if k == 0 else 2]:

            @pl.when(ok)
            def _():
                if arrive:
                    og_wait(zs * 4 + (1 - y) * 2 + c)
                cross(zs, act)

    own_sends(start)
    w_copies = []
    for d in range(1, n_rep):
        q = lax.rem(rep + d, n_rep)
        w_copies.append(remote(w_ref, wfull.at[rep], w_send.at[d], w_recv.at[rep], rep=q))
        w_copies[-1].start()

    def place_copy(d):
        e = lax.rem(me + d, n_ep)
        return remote(place_ref.at[e], place_all.at[me], pl_send.at[d], pl_recv.at[me], ep=e)

    @pl.loop(1, n_ep)
    def _(d):
        place_copy(d).start()

    def h_copy(e):
        return remote(hsend.at[e, pl.ds(0, sent)], hrecv.at[me, pl.ds(0, sent)], h_send.at[e], h_recv.at[me], ep=e)

    def r_copy(s):
        return remote(igbuf.at[s, pl.ds(0, sent)], returned_ref.at[me], r_send.at[s], r_recv.at[me], ep=s)

    def plane(k):
        return lax.rem(z + way * k + outer, outer)

    def hidden_group(k):
        first = plane(k) * 4
        ids = lax.broadcasted_iota(jnp.int32, (4 * cap, slot_ref.shape[1]), 0) + first * cap
        pick = jnp.where(ids == slot_ref[...], 1.0, 0.0).astype(jnp.bfloat16)
        got = jnp.dot(pick, gated_ref[...], preferred_element_type=jnp.float32)
        hsend[pl.ds(first, 4)] = got.astype(jnp.bfloat16).reshape(4, cap, inner)

        @pl.loop(0, 4)
        def _(i):
            e = first + i

            @pl.when(e != me)
            def _():
                h_copy(e).start()

            @pl.when(e == me)
            def _():
                hrecv[me] = hsend[me]

    hidden_group(0)
    for k in range(1, outer):
        forward(k, start, True)
        hidden_group(k)
        crossing(k - 1, start, True)
    crossing(outer - 1, start, True)

    for d in range(1, n_rep):
        q = lax.rem(rep + d, n_rep)
        remote(w_ref, wfull.at[q], w_send.at[d], w_recv.at[q], rep=q).wait_recv()

    @pl.loop(1, n_ep)
    def _(d):
        s = lax.rem(me + d, n_ep)
        remote(place_ref.at[s], place_all.at[s], pl_send.at[d], pl_recv.at[s], ep=s).wait_recv()

    @pl.loop(0, outer)
    def _(k):
        first = plane(k) * 4
        og_wait(first + 1 - c)
        og_wait(first + 3 - c)

        @pl.loop(0, 4)
        def _(i):
            s = first + i
            ids = lax.broadcasted_iota(jnp.int32, (cap, tok), 0)
            pick = jnp.where(ids == place_all[s][0:1, :], 1.0, 0.0).astype(jnp.bfloat16)
            got = jnp.dot(pick, og_all[s], preferred_element_type=jnp.float32)
            rows[pl.ds(pl.multiple_of(s * cap, 16), cap), :] = got.astype(jnp.bfloat16)

        here = rows[pl.ds(pl.multiple_of(first * cap, 16), 4 * cap), :]
        back = lax.dot_general(
            here,
            wfull[...].reshape(inner, width),
            (((1,), (1,)), ((), ())),
            preferred_element_type=jnp.float32,
        )
        igbuf[pl.ds(first, 4)] = back.astype(jnp.bfloat16).reshape(4, cap, inner)

        @pl.loop(0, 4)
        def _(i):
            s = first + i

            @pl.when(s != me)
            def _():
                r_copy(s).start()

    own = pltpu.make_async_copy(igbuf.at[me, pl.ds(0, sent)], returned_ref.at[me], r_recv.at[me])
    own.start()

    @pl.loop(1, n_ep)
    def _(d):
        s = lax.rem(me + d, n_ep)
        remote(hsend.at[s, pl.ds(0, sent)], hrecv.at[s, pl.ds(0, sent)], h_send.at[s], h_recv.at[s], ep=s).wait_recv()

    def g_copy(d, j, q, slot):
        cols = pl.ds(j * wide, wide)
        return remote(
            term.at[q, :, cols], parts.at[slot, :, cols],
            g_send.at[d, j], g_recv.at[slot, j], rep=q,
        )

    left = hrecv[...].reshape(n_ep * cap, inner)
    for j in range(chunks):
        cols = pl.ds(j * wide, wide)
        got = lax.dot_general(
            left, rows[:, cols], (((0,), (0,)), ((), ())), preferred_element_type=jnp.float32
        )
        term[:, :, cols] = got.astype(jnp.bfloat16).reshape(n_rep, own_rows, wide)
        for d in range(1, n_rep):
            g_copy(d, j, lax.rem(rep + d, n_rep), rep).start()

    total = jnp.zeros((own_rows, 1), jnp.float32)
    for j in range(chunks):
        cols = pl.ds(j * wide, wide)
        part = term[rep, :, cols].astype(jnp.float32)
        for d in range(1, n_rep):
            q = lax.rem(rep + d, n_rep)
            g_copy(d, j, q, q).wait_recv()
            part = part + parts[q, :, cols].astype(jnp.float32)
        grad[:, cols] = part
        square = part * part
        total = total + jnp.sum(square, axis=1, keepdims=True)
        coln_ref[:, cols] = decay_rate * colm_ref[:, cols] + (1.0 - decay_rate) * (
            jnp.sum(square, axis=0, keepdims=True) / own_rows + epsilon
        )
    row_new = decay_rate * rowm_ref[...] + (1.0 - decay_rate) * (total / width + epsilon)
    rown_ref[...] = row_new
    mean = jnp.sum(row_new, axis=0, keepdims=True) / own_rows
    for j in range(chunks):
        cols = pl.ds(j * wide, wide)
        second = row_new * coln_ref[:, cols] / mean
        update_ref[:, cols] = (grad[:, cols] * lax.rsqrt(second)).astype(jnp.bfloat16)

    own.wait()

    @pl.loop(1, n_ep)
    def _(d):
        s = lax.rem(me + d, n_ep)
        place_copy(d).wait_send()
        h_copy(s).wait_send()
        r_copy(s).wait_send()
        remote(igbuf.at[s, pl.ds(0, sent)], returned_ref.at[s], r_send.at[s], r_recv.at[s], ep=s).wait_recv()

    own_sends(finish)
    for k in range(1, outer):
        forward(k, finish, False)
        crossing(k - 1, finish, False)
    crossing(outer - 1, finish, False)
    for copy in w_copies:
        copy.wait_send()
    for j in range(chunks):
        for d in range(1, n_rep):
            g_copy(d, j, lax.rem(rep + d, n_rep), rep).wait_send()


def local(out_grad, hidden, expert_ids, gates, weights, row_moment, col_moment):
    tok, top = expert_ids.shape
    width = out_grad.shape[1]
    inner = hidden.shape[2]
    n_ep, n_rep = lax.axis_size("ep"), lax.axis_size("rep")
    capacity = max(2, tok * top * 9 // (8 * n_ep))
    sent, cap = up_to(capacity, 8), up_to(capacity, 16)
    outer = n_ep // 4
    own_rows = inner // n_rep
    routes = tok * top
    chunks = 4

    hit = expert_ids[:, :, None] == jnp.arange(n_ep, dtype=jnp.int32)
    chosen = jnp.any(hit, axis=1)
    before = jnp.tril(jnp.ones((tok, tok), jnp.bfloat16), -1)
    rank = jnp.dot(
        before, chosen.astype(jnp.bfloat16), preferred_element_type=jnp.float32
    ).astype(jnp.int32)
    place = jnp.where(chosen, rank, -1).T
    place = jnp.broadcast_to(place[:, None, :], (n_ep, 8, tok))
    rank_own = jnp.sum(jnp.where(hit, rank[:, None, :], 0), axis=2)
    slot = (expert_ids * cap + rank_own).reshape(1, routes)
    position = (expert_ids * sent + rank_own).reshape(routes)
    gated = (
        (gates[:, :, None] * hidden.astype(jnp.float32)).astype(jnp.bfloat16).reshape(routes, inner)
    )

    vmem = pl.BlockSpec(memory_space=pltpu.VMEM)
    anywhere = pl.BlockSpec(memory_space=pl.ANY)
    dma = pltpu.SemaphoreType.DMA
    returned, update, row_new, col_new = pl.pallas_call(
        functools.partial(kernel, (n_ep, n_rep, outer, sent, cap, chunks)),
        out_shape=(
            jax.ShapeDtypeStruct((n_ep, sent, inner), jnp.bfloat16),
            jax.ShapeDtypeStruct((own_rows, width), jnp.bfloat16),
            jax.ShapeDtypeStruct((own_rows, 1), jnp.float32),
            jax.ShapeDtypeStruct((1, width), jnp.float32),
        ),
        in_specs=[vmem] * 7,
        out_specs=(anywhere, vmem, vmem, vmem),
        scratch_shapes=[
            pltpu.VMEM((n_ep, tok, width), jnp.bfloat16),
            pltpu.VMEM((n_ep, 8, tok), jnp.int32),
            pltpu.VMEM((n_ep, cap, inner), jnp.bfloat16),
            pltpu.VMEM((n_ep, cap, inner), jnp.bfloat16),
            pltpu.VMEM((n_ep * cap, width), jnp.bfloat16),
            pltpu.VMEM((n_ep, cap, inner), jnp.bfloat16),
            pltpu.VMEM((n_rep, own_rows, width), jnp.bfloat16),
            pltpu.VMEM((n_rep, own_rows, width), jnp.bfloat16),
            pltpu.VMEM((own_rows, width), jnp.float32),
            dma((n_ep,)),
            dma((outer,)),
            dma((outer,)),
            dma((outer,)),
            dma((2 * outer,)),
            dma((n_ep,)),
            dma((n_ep,)),
            dma((n_ep,)),
            dma((n_ep,)),
            dma((n_ep,)),
            dma((n_ep,)),
            dma((n_rep,)),
            dma((n_rep,)),
            dma((n_rep, chunks)),
            dma((n_rep, chunks)),
        ],
        compiler_params=pltpu.CompilerParams(
            collective_id=0, has_side_effects=True, vmem_limit_bytes=67043328
        ),
    )(
        out_grad,
        gated,
        slot,
        place,
        weights[0],
        row_moment.reshape(own_rows, 1),
        col_moment.reshape(1, width),
    )

    back = returned.reshape(n_ep * sent, inner)[position].reshape(tok, top, inner)
    hidden_grad = (gates[:, :, None] * back.astype(jnp.float32)).astype(jnp.bfloat16)
    return (
        hidden_grad,
        update[None],
        row_new.reshape(1, own_rows),
        col_new.reshape(1, 1, width),
    )


def solution(mesh):
    return jax.shard_map(
        local,
        mesh=mesh,
        in_specs=(
            P(("ep", "rep"), None),
            P(("ep", "rep"), None, None),
            P(("ep", "rep"), None),
            P(("ep", "rep"), None),
            P("ep", "rep", None),
            P("ep", "rep"),
            P("ep", "rep", None),
        ),
        out_specs=(
            P(("ep", "rep"), None, None),
            P("ep", "rep", None),
            P("ep", "rep"),
            P("ep", "rep", None),
        ),
        check_vma=False,
    )
```

time: 235 us -> 148 us (0.63); the launches traced: 232 us -> 148 us
  waiting for transfers between devices: 152 us -> 0 us
  Pallas kernels: 0 us -> 127 us
  matrix products: 24.3 us -> 0.2 us
  starting transfers between devices: 18.6 us -> 0 us
  between operations: 14.5 us -> 0.71 us
  other arithmetic: 17.9 us -> 7.23 us
  local copies, waits for them, and re-layouts: 5 us -> 12.9 us
    pallas_call x0 -> x1, Pallas kernels: none -> 127 us  [local(): pl.pallas_call(functools.partial(kernel, (n_ep, n_rep, outer, sent, cap,...]
    all_gather x2 -> x0, waiting for transfers between devices: 112 us -> none  [the longest x1 79.4 us: local(): gathered = lax.all_gather(out_grad, 'ep', axis=0, tiled=False)]
    all_to_all x3 -> x0, waiting for transfers between devices: 38.8 us -> none  [the longest x1 38.8 us: local(): lax.all_to_all(input_grad, 'ep', split_axis=0, concat_axis=0, tiled=True)]
    dot_general x3 -> x0, matrix products: 23.5 us -> none  [the longest x1 8.42 us: local(): lax.dot_general(rows, weight, (((1,), (1,)), ((), ())), preferred_element...]
    all_to_all x3 -> x0, starting transfers between devices: 18.5 us -> none  [the longest x1 6.3 us: local(): lax.all_to_all(place, 'ep', split_axis=0, concat_axis=0, tiled=True)]
    scatter x1 -> x0, other arithmetic: 7.4 us -> none  [local(): jnp.zeros((slots, inner), jnp.bfloat16).at[position].set(gated)]
    broadcast_in_dim x1 -> x0, other arithmetic: 3.18 us -> none  [local(): return (hidden_grad, update[None], row_new[None], col_new[None, None])]
    reshape x0 -> x1, other arithmetic: none -> 2.88 us  [local(): (gates[:, :, None] * hidden.astype(jnp.float32)).astype(jnp.bfloat16)]
  transfers between devices with their start and end apart: 6 -> 0, of which waited for: 3 -> 0; matrix products, arithmetic and copies ran while one was open for 17% -> 0% of each run, Pallas kernels for 0% -> 0%
where the time goes in v2:
time: 148 us
  Pallas kernels  127 us (86%)
  local copies, waits for them, and re-layouts  12.9 us (9%)
  other arithmetic  7.23 us (5%)
    pallas_call x1, Pallas kernels, local(): pl.pallas_call(functools.partial(kernel, (n_ep, n_rep, outer, sent, cap,...  127 us
    gather x1, local copies, waits for them, and re-layouts, local(): returned.reshape(n_ep * sent, inner)[position].reshape(tok, top, inner)  6.7 us

profile of v2, /device:TPU:8, one launch (start us, length us, event | category | flops | bytes accessed | tf_op | source)
XLA Modules:
  0.0 147.8 jit_solution(8556089912432564343)
XLA Ops:
  0.6 0.7 fusion.2
  1.3 0.2 convolution_convert_fusion
  1.5 0.7 select_reduce_fusion
  2.3 0.7 multiply_add_fusion
  3.0 0.6 broadcast_in_dim.43.place_ref
  3.6 0.1 copy.24
  3.7 0.1 reshape.72
  3.8 0.6 broadcast_clamp_fusion
  4.4 0.8 copy.21
  5.2 0.0 copy-start.1
  5.2 0.1 copy.22
  5.3 0.7 reshape.68.slot_ref
  6.0 1.5 %copy.23.rowm_ref = f32[384,1]{1,0:T(8,128)} copy(f32[384,1]{0,1:T(1,128)} %bitcast.21) | data formatting | bytes 3072 | tf_op jit(solution)/shard_map/reshape | solution.py:390
  7.5 0.0 copy-done.1
  7.5 2.9 %fusion.1.gated_ref = bf16[1024,768]{1,0:T(8,128)(2,1)} fusion(bf16[128,8,768]{2,1,0:T(8,128)(2,1)} %param.8, f32[128,8]{1,0:T(8,128)S(1)} %copy.21), kind=kLoop, calls=%fused_computation.4 | loop fusion | flops 2359296 | bytes 3149824 | tf_op jit(solution)/shard_map/reshape | solution.py:339
  10.4 126.7 %shard_map.102 = (bf16[16,72,768]{2,1,0:T(8,128)(2,1)}, bf16[384,2048]{1,0:T(8,128)(2,1)}, f32[384,1]{1,0:T(8,128)}, f32[1,2048]{1,0:T(1,128)}) custom-call(bf16[128,2048]{1,0:T(8,128)(2,1)} %og_ref.1, bf16[1024,768]{1,0:T(8,128)(2,1)} %fusion.1.gated_ref, s32[1,1024]{1,0:T(1,128)} %reshape.68.slot_ref, s32[16,8,128]{2,1,0:T(8,128)} %broadcast_in_dim.43.place_ref, ...), custom_call_target="tpu_custom_call" | custom-call | tf_op jit(solution)/shard_map/pallas_call | solution.py:345
  137.1 0.0 copy-start.2
  137.1 6.7 %gather_fusion = bf16[1024,768]{1,0:T(8,128)(2,1)S(1)} fusion(bf16[1152,768]{1,0:T(8,128)(2,1)} %bitcast.15, s32[1024]{0:T(1024)} %broadcast_clamp_fusion), kind=kCustom, calls=%fused_computation | custom fusion | bytes 3149824 | tf_op jit(solution)/shard_map/gather | solution.py:394
  143.8 0.0 copy-done.2
  143.8 0.0 copy-start.3
  143.8 0.0 copy-start
  143.8 1.5 fusion
  145.3 0.0 copy-done.3
  145.3 0.1 reduce
  145.5 0.6 reshape.73
  146.0 0.0 copy-done
  146.0 0.0 copy-start.4
  146.0 1.1 copy.27
  147.2 0.0 copy-done.4
  147.2 0.6 copy.28
  (3 shorter events, 0.0 us)
Async XLA Ops:
  5.2 2.3 %copy-start.1 = (f32[128,8]{1,0:T(8,128)}, f32[128,8]{1,0:T(8,128)S(1)}, u32[]{:S(2)}) copy-start(f32[128,8]{1,0:T(8,128)S(1)} %copy.21) | copy-start | bytes 12292
  137.1 6.7 %copy-start.2 = (f32[128,8]{1,0:T(8,128)S(1)}, f32[128,8]{1,0:T(8,128)}, u32[]{:S(2)}) copy-start(f32[128,8]{1,0:T(8,128)} %copy-done.1) | copy-start | bytes 12292
  143.8 1.5 %copy-start.3 = (f32[384,1]{1,0:T(8,128)S(1)}, f32[384,1]{1,0:T(8,128)}, u32[]{:S(2)}) copy-start(f32[384,1]{1,0:T(8,128)} %get-tuple-element.10) | copy-start | bytes 4612
  143.8 2.2 %copy-start = (bf16[384,2048]{1,0:T(8,128)(2,1)S(1)}, bf16[384,2048]{1,0:T(8,128)(2,1)}, u32[]{:S(2)}) copy-start(bf16[384,2048]{1,0:T(8,128)(2,1)} %get-tuple-element.9) | copy-start | bytes 4718596
  146.0 1.1 copy-start.4

commit v3 on v2

--- a/solution.py
+++ b/solution.py
@@ -19,17 +19,21 @@
 def kernel(
     dims,
     og_ref,
-    gated_ref,
-    slot_ref,
-    place_ref,
+    hidden_ref,
+    ids_ref,
+    gates_ref,
     w_ref,
     rowm_ref,
     colm_ref,
     returned_ref,
+    out_ref,
     update_ref,
     rown_ref,
     coln_ref,
     og_all,
+    hid,
+    slot,
+    table,
     place_all,
     hsend,
     hrecv,
@@ -53,10 +57,12 @@
     w_recv,
     g_send,
     g_recv,
+    l_sem,
 ):
     n_ep, n_rep, outer, sent, cap, chunks = dims
     tok, width = og_ref.shape
-    inner = gated_ref.shape[1]
+    routes, inner = hidden_ref.shape
+    top = routes // tok
     own_rows = inner // n_rep
     wide = width // chunks
     term = wfull
@@ -67,11 +73,6 @@
     c_dev = z * 4 + y * 2 + (1 - c)
     way = 1 - 2 * (z // (outer // 2))
 
-    og_all[me] = og_ref[...]
-    wfull[rep] = w_ref[...]
-    place_all[me] = place_ref[me]
-    hrecv[...] = jnp.zeros_like(hrecv)
-
     barrier = pltpu.get_barrier_semaphore()
     for d in range(1, n_ep):
         pl.semaphore_signal(
@@ -154,15 +155,60 @@
                 cross(zs, act)
 
     own_sends(start)
+    own_og = pltpu.make_async_copy(og_ref, og_all.at[me], l_sem.at[0])
+    own_w = pltpu.make_async_copy(w_ref, wfull.at[rep], l_sem.at[1])
+    own_hidden = pltpu.make_async_copy(hidden_ref, hid, l_sem.at[2])
+    own_hidden.start()
+    own_og.start()
+    own_w.start()
     w_copies = []
     for d in range(1, n_rep):
         q = lax.rem(rep + d, n_rep)
         w_copies.append(remote(w_ref, wfull.at[rep], w_send.at[d], w_recv.at[rep], rep=q))
         w_copies[-1].start()
 
+    experts = lax.broadcasted_iota(jnp.int32, (tok, up_to(n_ep, 128)), 1)
+    chosen = jnp.zeros(experts.shape, jnp.float32)
+    gate = jnp.zeros(experts.shape, jnp.float32)
+    for k in range(top):
+        named = experts == ids_ref[:, k : k + 1]
+        chosen = jnp.where(named, 1.0, chosen)
+        gate = jnp.where(named, gates_ref[:, k : k + 1], gate)
+    row_i = lax.broadcasted_iota(jnp.int32, (tok, tok), 0)
+    col_i = lax.broadcasted_iota(jnp.int32, (tok, tok), 1)
+    earlier = jnp.where(row_i < col_i, 1.0, 0.0).astype(jnp.bfloat16)
+    rank = lax.dot_general(
+        chosen.T.astype(jnp.bfloat16), earlier, (((1,), (0,)), ((), ())),
+        preferred_element_type=jnp.float32,
+    )
+    place = jnp.where(chosen.T > 0.5, rank, -1.0)[:n_ep]
+    gate = gate.T[:n_ep]
+    first_row = lax.broadcasted_iota(jnp.int32, (n_ep, 8, tok), 1) == 0
+    table[...] = jnp.where(first_row, place[:, None, :], gate[:, None, :])
+    place_all[me] = table[me]
+    if cap > sent:
+        hrecv[:, sent:, :] = jnp.zeros((n_ep, cap - sent, inner), jnp.bfloat16)
+
+    spread = jnp.where(
+        lax.broadcasted_iota(jnp.int32, (tok, routes), 1) // top
+        == lax.broadcasted_iota(jnp.int32, (tok, routes), 0), 1.0, 0.0,
+    ).astype(jnp.bfloat16)
+    named = lax.dot_general(
+        ids_ref[...].astype(jnp.float32).astype(jnp.bfloat16), spread, (((0,), (0,)), ((), ())),
+        preferred_element_type=jnp.float32,
+    )
+    turn = lax.broadcasted_iota(jnp.int32, (top, routes), 1) % top
+    mine = turn == lax.broadcasted_iota(jnp.int32, (top, routes), 0)
+    named = jnp.sum(jnp.where(mine, named, 0.0), axis=0, keepdims=True)
+    ranks = jnp.dot(place.astype(jnp.bfloat16), spread, preferred_element_type=jnp.float32)
+    number = lax.broadcasted_iota(jnp.int32, (n_ep, routes), 0).astype(jnp.float32)
+    slot[...] = jnp.sum(
+        jnp.where(named == number, ranks + number * cap, 0.0), axis=0, keepdims=True
+    )
+
     def place_copy(d):
         e = lax.rem(me + d, n_ep)
-        return remote(place_ref.at[e], place_all.at[me], pl_send.at[d], pl_recv.at[me], ep=e)
+        return remote(table.at[e], place_all.at[me], pl_send.at[d], pl_recv.at[me], ep=e)
 
     @pl.loop(1, n_ep)
     def _(d):
@@ -177,11 +223,13 @@
     def plane(k):
         return lax.rem(z + way * k + outer, outer)
 
+    def slot_pick(first):
+        ids = lax.broadcasted_iota(jnp.int32, (4 * cap, routes), 0) + first * cap
+        return jnp.where(ids.astype(jnp.float32) == slot[...], 1.0, 0.0).astype(jnp.bfloat16)
+
     def hidden_group(k):
         first = plane(k) * 4
-        ids = lax.broadcasted_iota(jnp.int32, (4 * cap, slot_ref.shape[1]), 0) + first * cap
-        pick = jnp.where(ids == slot_ref[...], 1.0, 0.0).astype(jnp.bfloat16)
-        got = jnp.dot(pick, gated_ref[...], preferred_element_type=jnp.float32)
+        got = jnp.dot(slot_pick(first), hid[...], preferred_element_type=jnp.float32)
         hsend[pl.ds(first, 4)] = got.astype(jnp.bfloat16).reshape(4, cap, inner)
 
         @pl.loop(0, 4)
@@ -196,6 +244,7 @@
             def _():
                 hrecv[me] = hsend[me]
 
+    own_hidden.wait()
     hidden_group(0)
     for k in range(1, outer):
         forward(k, start, True)
@@ -210,7 +259,10 @@
     @pl.loop(1, n_ep)
     def _(d):
         s = lax.rem(me + d, n_ep)
-        remote(place_ref.at[s], place_all.at[s], pl_send.at[d], pl_recv.at[s], ep=s).wait_recv()
+        remote(table.at[s], place_all.at[s], pl_send.at[d], pl_recv.at[s], ep=s).wait_recv()
+
+    own_og.wait()
+    own_w.wait()
 
     @pl.loop(0, outer)
     def _(k):
@@ -221,9 +273,13 @@
         @pl.loop(0, 4)
         def _(i):
             s = first + i
-            ids = lax.broadcasted_iota(jnp.int32, (cap, tok), 0)
-            pick = jnp.where(ids == place_all[s][0:1, :], 1.0, 0.0).astype(jnp.bfloat16)
-            got = jnp.dot(pick, og_all[s], preferred_element_type=jnp.float32)
+            info = place_all[s]
+            ids = lax.broadcasted_iota(jnp.int32, (cap, tok), 0).astype(jnp.float32)
+            pick = jnp.where(ids == info[0:1, :], 1.0, 0.0)
+            factor = jnp.sum(pick * info[1:2, :], axis=1, keepdims=True)
+            got = factor * jnp.dot(
+                pick.astype(jnp.bfloat16), og_all[s], preferred_element_type=jnp.float32
+            )
             rows[pl.ds(pl.multiple_of(s * cap, 16), cap), :] = got.astype(jnp.bfloat16)
 
         here = rows[pl.ds(pl.multiple_of(first * cap, 16), 4 * cap), :]
@@ -267,6 +323,39 @@
         term[:, :, cols] = got.astype(jnp.bfloat16).reshape(n_rep, own_rows, wide)
         for d in range(1, n_rep):
             g_copy(d, j, lax.rem(rep + d, n_rep), rep).start()
+
+    def back_copy(first):
+        return pltpu.make_async_copy(
+            returned_ref.at[pl.ds(first, 4)], hsend.at[pl.ds(first, 4), pl.ds(0, sent)], l_sem.at[0]
+        )
+
+    def collect(k):
+        first = plane(k) * 4
+
+        @pl.loop(0, 4)
+        def _(i):
+            s = first + i
+
+            @pl.when(s != me)
+            def _():
+                h_copy(s).wait_send()
+                remote(
+                    igbuf.at[s, pl.ds(0, sent)], returned_ref.at[s], r_send.at[s], r_recv.at[s], ep=s
+                ).wait_recv()
+
+        back_copy(first).start()
+        back_copy(first).wait()
+        got = lax.dot_general(
+            slot_pick(first),
+            hsend[pl.ds(first, 4)].reshape(4 * cap, inner),
+            (((0,), (0,)), ((), ())),
+            preferred_element_type=jnp.float32,
+        ).astype(jnp.bfloat16)
+        out_ref[...] = got if k == 0 else out_ref[...] + got
+
+    own.wait()
+    for k in range(outer - 1):
+        collect(k)
 
     total = jnp.zeros((own_rows, 1), jnp.float32)
     for j in range(chunks):
@@ -282,23 +371,25 @@
         coln_ref[:, cols] = decay_rate * colm_ref[:, cols] + (1.0 - decay_rate) * (
             jnp.sum(square, axis=0, keepdims=True) / own_rows + epsilon
         )
-    row_new = decay_rate * rowm_ref[...] + (1.0 - decay_rate) * (total / width + epsilon)
-    rown_ref[...] = row_new
+    diagonal = lax.broadcasted_iota(jnp.int32, (own_rows, own_rows), 0) == (
+        lax.broadcasted_iota(jnp.int32, (own_rows, own_rows), 1)
+    )
+    rowm = jnp.sum(jnp.where(diagonal, rowm_ref[...], 0.0), axis=1, keepdims=True)
+    row_new = decay_rate * rowm + (1.0 - decay_rate) * (total / width + epsilon)
+    rown_ref[...] = jnp.sum(jnp.where(diagonal, row_new, 0.0), axis=0, keepdims=True)
     mean = jnp.sum(row_new, axis=0, keepdims=True) / own_rows
     for j in range(chunks):
         cols = pl.ds(j * wide, wide)
         second = row_new * coln_ref[:, cols] / mean
         update_ref[:, cols] = (grad[:, cols] * lax.rsqrt(second)).astype(jnp.bfloat16)
 
-    own.wait()
+    collect(outer - 1)
 
     @pl.loop(1, n_ep)
     def _(d):
         s = lax.rem(me + d, n_ep)
         place_copy(d).wait_send()
-        h_copy(s).wait_send()
         r_copy(s).wait_send()
-        remote(igbuf.at[s, pl.ds(0, sent)], returned_ref.at[s], r_send.at[s], r_recv.at[s], ep=s).wait_recv()
 
     own_sends(finish)
     for k in range(1, outer):
@@ -324,37 +415,26 @@
     routes = tok * top
     chunks = 4
 
-    hit = expert_ids[:, :, None] == jnp.arange(n_ep, dtype=jnp.int32)
-    chosen = jnp.any(hit, axis=1)
-    before = jnp.tril(jnp.ones((tok, tok), jnp.bfloat16), -1)
-    rank = jnp.dot(
-        before, chosen.astype(jnp.bfloat16), preferred_element_type=jnp.float32
-    ).astype(jnp.int32)
-    place = jnp.where(chosen, rank, -1).T
-    place = jnp.broadcast_to(place[:, None, :], (n_ep, 8, tok))
-    rank_own = jnp.sum(jnp.where(hit, rank[:, None, :], 0), axis=2)
-    slot = (expert_ids * cap + rank_own).reshape(1, routes)
-    position = (expert_ids * sent + rank_own).reshape(routes)
-    gated = (
-        (gates[:, :, None] * hidden.astype(jnp.float32)).astype(jnp.bfloat16).reshape(routes, inner)
-    )
-
     vmem = pl.BlockSpec(memory_space=pltpu.VMEM)
     anywhere = pl.BlockSpec(memory_space=pl.ANY)
     dma = pltpu.SemaphoreType.DMA
-    returned, update, row_new, col_new = pl.pallas_call(
+    _, hidden_grad, update, row_new, col_new = pl.pallas_call(
         functools.partial(kernel, (n_ep, n_rep, outer, sent, cap, chunks)),
         out_shape=(
             jax.ShapeDtypeStruct((n_ep, sent, inner), jnp.bfloat16),
+            jax.ShapeDtypeStruct((routes, inner), jnp.bfloat16),
             jax.ShapeDtypeStruct((own_rows, width), jnp.bfloat16),
-            jax.ShapeDtypeStruct((own_rows, 1), jnp.float32),
+            jax.ShapeDtypeStruct((1, own_rows), jnp.float32),
             jax.ShapeDtypeStruct((1, width), jnp.float32),
         ),
-        in_specs=[vmem] * 7,
-        out_specs=(anywhere, vmem, vmem, vmem),
+        in_specs=[anywhere, anywhere, vmem, vmem, anywhere, vmem, vmem],
+        out_specs=(anywhere, vmem, vmem, vmem, vmem),
         scratch_shapes=[
             pltpu.VMEM((n_ep, tok, width), jnp.bfloat16),
-            pltpu.VMEM((n_ep, 8, tok), jnp.int32),
+            pltpu.VMEM((routes, inner), jnp.bfloat16),
+            pltpu.VMEM((1, routes), jnp.float32),
+            pltpu.VMEM((n_ep, 8, tok), jnp.float32),
+            pltpu.VMEM((n_ep, 8, tok), jnp.float32),
             pltpu.VMEM((n_ep, cap, inner), jnp.bfloat16),
             pltpu.VMEM((n_ep, cap, inner), jnp.bfloat16),
             pltpu.VMEM((n_ep * cap, width), jnp.bfloat16),
@@ -377,24 +457,23 @@
             dma((n_rep,)),
             dma((n_rep, chunks)),
             dma((n_rep, chunks)),
+            dma((3,)),
         ],
         compiler_params=pltpu.CompilerParams(
             collective_id=0, has_side_effects=True, vmem_limit_bytes=67043328
         ),
     )(
         out_grad,
-        gated,
-        slot,
-        place,
+        hidden.reshape(routes, inner),
+        expert_ids,
+        gates,
         weights[0],
-        row_moment.reshape(own_rows, 1),
+        row_moment.reshape(1, own_rows),
         col_moment.reshape(1, width),
     )
 
-    back = returned.reshape(n_ep * sent, inner)[position].reshape(tok, top, inner)
-    hidden_grad = (gates[:, :, None] * back.astype(jnp.float32)).astype(jnp.bfloat16)
     return (
-        hidden_grad,
+        hidden_grad.reshape(tok, top, inner),
         update[None],
         row_new.reshape(1, own_rows),
         col_new.reshape(1, 1, width),

time: 148 us -> 137 us (0.926)
  other arithmetic: 7.23 us -> 0 us
  local copies, waits for them, and re-layouts: 12.9 us -> 7.92 us
    gather x1 -> x0, local copies, waits for them, and re-layouts: 6.7 us -> none  [local(): returned.reshape(n_ep * sent, inner)[position].reshape(tok, top, inner)]
    unnamed x13 -> x12, local copies, waits for them, and re-layouts: 2.55 us -> 7.92 us
    reshape x1 -> x0, other arithmetic: 2.88 us -> none  [local(): (gates[:, :, None] * hidden.astype(jnp.float32)).astype(jnp.bfloat16)]
    reshape x4 -> x0, local copies, waits for them, and re-layouts: 2.87 us -> none  [the longest x1 1.5 us: local(): row_moment.reshape(own_rows, 1)]
    pallas_call x1, Pallas kernels: 127 us -> 128 us  [local(): pl.pallas_call(functools.partial(kernel, (n_ep, n_rep, outer, sent, cap,...]
where the time goes in v3:
time: 137 us
  Pallas kernels  128 us (93%)
  local copies, waits for them, and re-layouts  7.92 us (6%)
    pallas_call x1, Pallas kernels, local(): pl.pallas_call(functools.partial(kernel, (n_ep, n_rep, outer, sent, cap,...  128 us
    unnamed x12, local copies, waits for them, and re-layouts  7.92 us

profile of v3, /device:TPU:8, one launch (start us, length us, event | category | flops | bytes accessed | tf_op | source)
XLA Modules:
  0.0 136.8 jit_solution(10673418931601055241)
XLA Ops:
  0.6 1.4 %copy.11.ids_ref = s32[128,8]{1,0:T(8,128)} copy(s32[128,8]{0,1:T(8,128)} %param.9) | data formatting | bytes 8192 | tf_op args[2]
  2.0 1.4 %copy.12.gates_ref = f32[128,8]{1,0:T(8,128)} copy(f32[128,8]{0,1:T(8,128)} %param.10) | data formatting | bytes 8192 | tf_op args[3]
  3.5 128.2 %shard_map.102 = (bf16[16,72,768]{2,1,0:T(8,128)(2,1)}, bf16[1024,768]{1,0:T(8,128)(2,1)}, bf16[384,2048]{1,0:T(8,128)(2,1)}, f32[1,384]{1,0:T(1,128)}, f32[1,2048]{1,0:T(1,128)}) custom-call(bf16[128,2048]{1,0:T(8,128)(2,1)} %og_ref.1, bf16[1024,768]{1,0:T(8,128)(2,1)} %bitcast.6, s32[128,8]{1,0:T(8,128)} %copy.11.ids_ref, f32[128,8]{1,0:T(8,128)} %copy.12.gates_ref, ...), custom_call_target="tpu_custom_call" | custom-call | tf_op jit(solution)/shard_map/pallas_call | solution.py:421
  131.7 0.0 copy-start
  131.7 2.8 %copy.17 = bf16[128,8,768]{2,1,0:T(8,128)(2,1)} copy(bf16[128,8,768]{2,1,0:T(8,128)(2,1)} %bitcast.9) | data formatting | bytes 3145728
  134.5 0.0 copy-done
  134.5 0.0 copy-start.2
  134.5 0.0 copy-start.1
  134.5 1.1 copy.18
  135.6 0.0 copy-done.2
  135.6 0.6 copy.19
  136.2 0.0 copy-done.1
  136.2 0.6 copy.20
Async XLA Ops:
  131.7 2.8 %copy-start = (bf16[384,2048]{1,0:T(8,128)(2,1)S(1)}, bf16[384,2048]{1,0:T(8,128)(2,1)}, u32[]{:S(2)}) copy-start(bf16[384,2048]{1,0:T(8,128)(2,1)} %get-tuple-element.9) | copy-start | bytes 4718596
  134.5 1.1 copy-start.2
  134.5 1.7 %copy-start.1 = (f32[1,2048]{1,0:T(1,128)S(1)}, f32[1,2048]{1,0:T(1,128)}, u32[]{:S(2)}) copy-start(f32[1,2048]{1,0:T(1,128)} %get-tuple-element.11) | copy-start | bytes 24580

commit v4 on v3

--- a/solution.py
+++ b/solution.py
@@ -167,22 +167,21 @@
         w_copies.append(remote(w_ref, wfull.at[rep], w_send.at[d], w_recv.at[rep], rep=q))
         w_copies[-1].start()
 
-    experts = lax.broadcasted_iota(jnp.int32, (tok, up_to(n_ep, 128)), 1)
+    experts = lax.broadcasted_iota(jnp.int32, (n_ep, tok), 0)
     chosen = jnp.zeros(experts.shape, jnp.float32)
     gate = jnp.zeros(experts.shape, jnp.float32)
     for k in range(top):
-        named = experts == ids_ref[:, k : k + 1]
+        named = experts == ids_ref[k : k + 1, :]
         chosen = jnp.where(named, 1.0, chosen)
-        gate = jnp.where(named, gates_ref[:, k : k + 1], gate)
+        gate = jnp.where(named, gates_ref[k : k + 1, :], gate)
     row_i = lax.broadcasted_iota(jnp.int32, (tok, tok), 0)
     col_i = lax.broadcasted_iota(jnp.int32, (tok, tok), 1)
     earlier = jnp.where(row_i < col_i, 1.0, 0.0).astype(jnp.bfloat16)
     rank = lax.dot_general(
-        chosen.T.astype(jnp.bfloat16), earlier, (((1,), (0,)), ((), ())),
+        chosen.astype(jnp.bfloat16), earlier, (((1,), (0,)), ((), ())),
         preferred_element_type=jnp.float32,
     )
-    place = jnp.where(chosen.T > 0.5, rank, -1.0)[:n_ep]
-    gate = gate.T[:n_ep]
+    place = jnp.where(chosen > 0.5, rank, -1.0)
     first_row = lax.broadcasted_iota(jnp.int32, (n_ep, 8, tok), 1) == 0
     table[...] = jnp.where(first_row, place[:, None, :], gate[:, None, :])
     place_all[me] = table[me]
@@ -194,7 +193,7 @@
         == lax.broadcasted_iota(jnp.int32, (tok, routes), 0), 1.0, 0.0,
     ).astype(jnp.bfloat16)
     named = lax.dot_general(
-        ids_ref[...].astype(jnp.float32).astype(jnp.bfloat16), spread, (((0,), (0,)), ((), ())),
+        ids_ref[...].astype(jnp.float32).astype(jnp.bfloat16), spread, (((1,), (0,)), ((), ())),
         preferred_element_type=jnp.float32,
     )
     turn = lax.broadcasted_iota(jnp.int32, (top, routes), 1) % top
@@ -250,7 +249,6 @@
         forward(k, start, True)
         hidden_group(k)
         crossing(k - 1, start, True)
-    crossing(outer - 1, start, True)
 
     for d in range(1, n_rep):
         q = lax.rem(rep + d, n_rep)
@@ -266,6 +264,10 @@
 
     @pl.loop(0, outer)
     def _(k):
+        @pl.when(k == outer - 1)
+        def _():
+            crossing(outer - 1, start, True)
+
         first = plane(k) * 4
         og_wait(first + 1 - c)
         og_wait(first + 3 - c)
@@ -465,8 +467,8 @@
     )(
         out_grad,
         hidden.reshape(routes, inner),
-        expert_ids,
-        gates,
+        expert_ids.T,
+        gates.T,
         weights[0],
         row_moment.reshape(1, own_rows),
         col_moment.reshape(1, width),

time: 137 us -> 144 us (1.051)
  the two profiles are of different devices: /device:TPU:8 before, /device:TPU:5 now
where the time goes in v4:
time: 144 us; the launch traced here: 143 us
  Pallas kernels  138 us (96%)
  local copies, waits for them, and re-layouts  5.08 us (4%)
    pallas_call x1, Pallas kernels, local(): pl.pallas_call(functools.partial(kernel, (n_ep, n_rep, outer, sent, cap,...  138 us
    unnamed x10, local copies, waits for them, and re-layouts  5.08 us

profile of v4, /device:TPU:5, one launch (start us, length us, event | category | flops | bytes accessed | tf_op | source)
XLA Modules:
  0.0 143.5 jit_solution(15114784482527939520)
XLA Ops:
  0.6 137.7 %shard_map.102 = (bf16[16,72,768]{2,1,0:T(8,128)(2,1)}, bf16[1024,768]{1,0:T(8,128)(2,1)}, bf16[384,2048]{1,0:T(8,128)(2,1)}, f32[1,384]{1,0:T(1,128)}, f32[1,2048]{1,0:T(1,128)}) custom-call(bf16[128,2048]{1,0:T(8,128)(2,1)} %og_ref.1, bf16[1024,768]{1,0:T(8,128)(2,1)} %bitcast.8, s32[8,128]{1,0:T(8,128)} %bitcast.14, f32[8,128]{1,0:T(8,128)} %bitcast.15, ...), custom_call_target="tpu_custom_call" | custom-call | tf_op jit(solution)/shard_map/pallas_call | solution.py:423
  138.4 0.0 copy-start
  138.4 2.8 %copy.15 = bf16[128,8,768]{2,1,0:T(8,128)(2,1)} copy(bf16[128,8,768]{2,1,0:T(8,128)(2,1)} %bitcast.11) | data formatting | bytes 3145728
  141.2 0.0 copy-done
  141.2 0.0 copy-start.2
  141.2 0.0 copy-start.1
  141.2 1.1 copy.16
  142.3 0.0 copy-done.2
  142.3 0.6 copy.17
  142.9 0.0 copy-done.1
  142.9 0.6 copy.18
Async XLA Ops:
  138.4 2.8 %copy-start = (bf16[384,2048]{1,0:T(8,128)(2,1)S(1)}, bf16[384,2048]{1,0:T(8,128)(2,1)}, u32[]{:S(2)}) copy-start(bf16[384,2048]{1,0:T(8,128)(2,1)} %get-tuple-element.9) | copy-start | bytes 4718596
  141.2 1.1 copy-start.2
  141.2 1.7 %copy-start.1 = (f32[1,2048]{1,0:T(1,128)S(1)}, f32[1,2048]{1,0:T(1,128)}, u32[]{:S(2)}) copy-start(f32[1,2048]{1,0:T(1,128)} %get-tuple-element.11) | copy-start | bytes 24580
